TPU v7x, 128 devices: a whole 4x4x4 slice. The times are simulated.
128 devices in a mesh: shard: 64 (over z, y, x), rep: 2 (over core).
Axes of the slice: x: 4, y: 4, z: 4, core: 2. Of those that a mesh axis runs over, the one named last changes fastest.
Arguments:
- user_emb: bfloat16 [1024, 1024, 256], P('shard', 'rep'), may hold values from -6 to 6
- elig_owner: int32 [1024, 4], P('shard'), may hold values from 0 to 63, all different within a row; in each aligned block of 16 rows (0 to 15, 16 to 31, ...) at most 2 rows name the same one
- elig_local: int32 [1024, 4], P('shard'), may hold values from 0 to 127
- cluster_size: int32 [1024], P('shard'), may hold values from 1 to 1024, 655360 in all
- camp_emb: bfloat16 [8192, 128, 256], P('shard'), may hold values from -6 to 6
- camp_count: int32 [8192], P('shard'), may hold values from 1 to 128, 786432 in all
- dual_init: float32 [8192, 128], P('shard'), may hold values from 0 to 2
- spend_limit: float32 [8192, 128], P('shard'), may hold values from 0.1 to 10
Outputs:
- user_dual: float32 [1024, 1024], P('shard', 'rep')
- campaign_dual: float32 [8192, 128], P('shard')
Inputs may be any that keep to these rules, and one draw needn't show every extreme that they name: `elig_owner`: each row names 4 different owners; among the 16 rows of one shard index no owner is named more than 2 times.
All inputs are finite; a program needn't handle non-finite values. No bound on the sum of `cluster_size` or of `camp_count` on one device may be relied on, other than what follows from the above.
Results may differ from a plain program's by a relative error of at most 0.0015.
Values may be sent and summed in bfloat16 or wider, within the bound.
A program may use at most 128 MiB of HBM per device.

v0:
```python
import jax
import jax.numpy as jnp
from jax import lax
from jax.sharding import PartitionSpec as P

epsilon = 1e-06
temper = 0.25
sharpness = 16.0


def body(
    user_emb, elig_owner, elig_local, cluster_size, camp_emb, camp_count, dual_init, spend_limit
):
    shard_count = lax.axis_size("shard")
    replica = lax.axis_index("rep")
    clusters, user_slots, emb_width = user_emb.shape
    blocks_here, block_camps, _ = camp_emb.shape
    fanout = elig_owner.shape[1]
    n_items = clusters * fanout
    capacity = 2 * n_items // shard_count
    n_slots = shard_count * capacity
    owners = elig_owner.reshape(-1)
    local_ids = elig_local.reshape(-1)
    owner_hot = (owners[:, None] == jnp.arange(shard_count, dtype=jnp.int32)[None, :]).astype(
        jnp.int32
    )
    before = jnp.cumsum(owner_hot, axis=0) - owner_hot
    slot_rank = jnp.sum(before * owner_hot, axis=1)
    item_slot = owners * capacity + slot_rank
    slot_hit = item_slot[:, None] == jnp.arange(n_slots, dtype=jnp.int32)[None, :]
    wanted = jnp.sum(jnp.where(slot_hit, local_ids[:, None], 0), axis=0).reshape(
        shard_count, capacity
    )
    incoming = lax.all_to_all(wanted, "shard", split_axis=0, concat_axis=0, tiled=True)
    reply_rows = jnp.take(camp_emb, incoming, axis=0)
    reply_counts = jnp.take(camp_count, incoming, axis=0).astype(jnp.bfloat16)
    got_rows, got_counts = (
        lax.all_to_all(reply_rows, "shard", split_axis=0, concat_axis=0, tiled=True),
        lax.all_to_all(reply_counts, "shard", split_axis=0, concat_axis=0, tiled=True),
    )
    fetched = got_rows.reshape(n_slots, block_camps, emb_width)
    item_emb = jnp.take(fetched, item_slot, axis=0).reshape(
        clusters, fanout, block_camps, emb_width
    )
    item_count = jnp.take(got_counts.reshape(n_slots), item_slot, axis=0).astype(jnp.float32)
    live_camps = (
        jnp.arange(block_camps, dtype=jnp.float32)[None, None, :]
        < item_count.reshape(clusters, fanout)[:, :, None]
    )
    camp_scale = lax.rsqrt(jnp.mean(jnp.square(item_emb.astype(jnp.float32)), axis=-1) + epsilon)
    user_scale = lax.rsqrt(jnp.mean(jnp.square(user_emb.astype(jnp.float32)), axis=-1) + epsilon)
    positions = replica * user_slots + jnp.arange(user_slots, dtype=jnp.int32)
    live_users = positions[None, :] < cluster_size[:, None]

    def affinity():
        raw_dots = jnp.einsum(
            "kuh,kech->keuc", user_emb, item_emb, preferred_element_type=jnp.float32
        )
        return (
            raw_dots
            * (sharpness / emb_width)
            * user_scale[:, None, :, None]
            * camp_scale[:, :, None, :]
        )

    def allocate(item_duals):
        scores = affinity()
        weights = jnp.where(
            live_camps[:, :, None, :], jnp.exp((scores - item_duals[:, :, None, :]) / temper), 0.0
        )
        denominator = 1.0 + jnp.sum(weights, axis=(1, 3))
        return (weights, denominator)

    def fetch_duals(duals):
        outgoing = jnp.take(duals, incoming, axis=0)
        reply_duals = lax.all_to_all(
            outgoing.astype(jnp.bfloat16), "shard", split_axis=0, concat_axis=0, tiled=True
        ).astype(outgoing.dtype)
        flat_duals = reply_duals.reshape(n_slots, block_camps)
        return jnp.take(flat_duals, item_slot, axis=0).reshape(clusters, fanout, block_camps)

    block_hit = (
        jnp.arange(blocks_here, dtype=jnp.int32)[:, None] == incoming.reshape(-1)[None, :]
    ).astype(jnp.float32)

    def new_duals(duals):
        weights, denominator = allocate(fetch_duals(duals))
        alloc_share = weights / denominator[:, None, :, None]
        spend_items = jnp.sum(
            jnp.where(live_users[:, None, :, None], alloc_share, 0.0), axis=2
        ).reshape(n_items, block_camps)
        spend_slots = jnp.dot(
            slot_hit.T.astype(jnp.float32), spend_items, precision=lax.Precision.HIGHEST
        )
        spend_slots = spend_slots.reshape(shard_count, capacity, block_camps)
        arrived = lax.all_to_all(
            spend_slots.astype(jnp.bfloat16), "shard", split_axis=0, concat_axis=0, tiled=True
        ).astype(spend_slots.dtype)
        own_spend = jnp.dot(
            block_hit, arrived.reshape(-1, block_camps), precision=lax.Precision.HIGHEST
        )
        spend_total = lax.psum(own_spend.astype(jnp.bfloat16), "rep").astype(jnp.float32)
        return jnp.maximum(
            0.0, duals + temper * jnp.log((spend_total + spend_limit) / (2.0 * spend_limit))
        )

    duals_one = new_duals(dual_init)
    duals_two = new_duals(duals_one)
    weights, denominator = allocate(fetch_duals(duals_two))
    user_dual = jnp.where(live_users, temper * jnp.log(denominator), 0.0)
    return (user_dual, duals_two)


def solution(mesh):
    return jax.shard_map(
        body,
        mesh=mesh,
        in_specs=(
            P("shard", "rep", None),
            P("shard", None),
            P("shard", None),
            P("shard"),
            P("shard", None, None),
            P("shard"),
            P("shard", None),
            P("shard", None),
        ),
        out_specs=(P("shard", "rep"), P("shard", None)),
        check_vma=False,
    )
```

profile of v0, /device:TPU:1, one launch (start us, length us, event | category | flops | bytes accessed | tf_op | source)
XLA Modules:
  0.0 313.3 jit_solution(14749126904358895577)
XLA Ops:
  0.6 0.8 copy.78
  1.4 0.1 eq.66
  1.5 0.8 copy.80
  2.3 0.1 broadcast_in_dim.126
  2.4 0.1 reduce_window_sum.11
  2.5 0.2 select_reduce_fusion.2
  2.7 0.1 select_reduce_fusion.1
  2.8 0.1 all_to_all.32
  3.0 20.2 %all_to_all.51 = s32[64,1,2]{2,1,0:T(1,128)S(1)} all-to-all(s32[64,1,2]{2,1,0:T(1,128)S(1)} %bitcast.86), channel_id=1, replica_groups=mesh['shard'=64,'rep'=2] {'shard'}, dimensions={0} | all-to-all | bytes 1024 | tf_op jit(solution)/shard_map/all_to_all | solution.py:34
  23.2 0.1 copy.90
  23.4 0.1 copy.93
  23.4 0.1 reshape.350
  23.6 0.1 copy.86
  23.7 0.1 reshape.308
  23.9 1.2 gather_fusion
  25.1 0.1 gather.29
  25.3 0.8 copy.88
  26.1 4.7 %all-to-all-start.1 = ((bf16[64,1,2]{2,1,0:T(2,128)(2,1)}), bf16[64,1,2]{2,1,0:T(2,128)(2,1)S(1)}, u32[]{:S(2)}, u32[]{:S(2)}) async-start(bf16[64,1,2]{2,1,0:T(2,128)(2,1)} %copy.88), calls=%async_computation.1 | async-start | bytes 65536 | tf_op jit(solution)/shard_map/all_to_all | solution.py:39
  30.8 0.7 gather_fusion.4
  31.4 0.8 select_convert_fusion.2
  32.2 9.8 %gather_fusion.2 = bf16[128,128,256]{2,1,0:T(8,128)(2,1)} fusion(bf16[128,128,256]{2,1,0:T(8,128)(2,1)} %param.16, s32[1024]{0:T(1024)S(1)} %pad_clamp_fusion.3), kind=kCustom, calls=%fused_computation.8 | custom fusion | bytes 16777728 | tf_op jit(solution)/shard_map/jit(_take)/gather | solution.py:35
  42.0 9.8 %all-to-all-start.3 = ((bf16[64,2,128]{2,1,0:T(2,128)(2,1)}), bf16[64,2,128]{2,1,0:T(2,128)(2,1)S(1)}, u32[]{:S(2)}, u32[]{:S(2)}) async-start(bf16[64,2,128]{2,1,0:T(2,128)(2,1)} %select_convert_fusion.2), calls=%async_computation.3 | async-start | bytes 65536 | tf_op jit(solution)/shard_map/all_to_all | solution.py:76
  51.8 7.4 %broadcast_select_fusion = bf16[64,2,128,256]{3,2,1,0:T(8,128)(2,1)} fusion(bf16[64,2,128,256]{3,2,1,0:T(8,128)(2,1)} %bitcast.64, pred[64,2]{1,0:T(8,128)(4,1)S(1)} %copy.90), kind=kLoop, calls=%fused_computation.24 | loop fusion | flops 4194304 | bytes 16777344 | tf_op jit(solution)/shard_map/jit(_take)/select_n | solution.py:35
  59.2 0.9 all-to-all-done.3
  60.1 9.3 %all-to-all-start.2 = ((bf16[64,2,128,256]{3,2,1,0:T(8,128)(2,1)}), bf16[64,2,128,256]{3,2,1,0:T(8,128)(2,1)}, u32[]{:S(2)}, u32[]{:S(2)}) async-start(bf16[64,2,128,256]{3,2,1,0:T(8,128)(2,1)} %broadcast_select_fusion), calls=%async_computation.2 | async-start | bytes 16777216 | tf_op jit(solution)/shard_map/all_to_all | solution.py:38
  69.5 0.1 mul.97
  69.8 3.3 %multiply_reduce_fusion.1 = f32[16,512]{1,0:T(8,128)S(1)} fusion(bf16[16,512,256]{2,1,0:T(8,128)(2,1)} %param.12), kind=kLoop, calls=%fused_computation.23 | loop fusion | flops 6283264 | bytes 4227072 | tf_op jit(solution)/shard_map/reduce_sum | solution.py:51
  73.1 0.1 reduce.2
  73.2 0.1 reshape.240
  73.4 0.8 gather_fusion.1
  74.2 0.1 gather.31
  74.4 0.6 gather_fusion.5
  75.1 100.4 %all-to-all-done.2 = bf16[64,2,128,256]{3,2,1,0:T(8,128)(2,1)} async-done(((bf16[64,2,128,256]{3,2,1,0:T(8,128)(2,1)}), bf16[64,2,128,256]{3,2,1,0:T(8,128)(2,1)}, u32[]{:S(2)}, u32[]{:S(2)}) %all-to-all-start.2) | async-done | bytes 8388640 | tf_op jit(solution)/shard_map/all_to_all | solution.py:38
  175.4 6.2 %gather_fusion.3 = bf16[64,128,256]{2,1,0:T(8,128)(2,1)} fusion(bf16[128,128,256]{2,1,0:T(8,128)(2,1)} %bitcast.6, s32[1024]{0:T(1024)S(1)} %pad_clamp_fusion.2), kind=kCustom, calls=%fused_computation.9 | custom fusion | bytes 8388864 | tf_op jit(solution)/shard_map/jit(_take)/gather | solution.py:42
  181.6 3.5 %multiply_reduce_fusion = f32[64,128]{1,0:T(8,128)S(1)} fusion(bf16[64,128,256]{2,1,0:T(8,128)(2,1)} %gather_fusion.3, pred[64]{0:T(512)(128)(4,1)S(1)} %get-tuple-element.6), kind=kLoop, calls=%fused_computation.22 | loop fusion | flops 8380416 | bytes 4227136 | tf_op jit(solution)/shard_map/reduce_sum | solution.py:50
  185.1 9.2 %bitcast_reduce_fusion.1 = (f32[16,512]{1,0:T(8,128)S(1)}, f32[16,4,128,512]{3,2,1,0:T(8,128)S(1)}) fusion(f32[16,4,128]{2,1,0:T(4,128)S(1)} %bitcast.73, f32[16,4,128]{2,1,0:T(4,128)S(1)} %bitcast.66, f32[16,512]{1,0:T(8,128)S(1)} %rsqrt_multiply_fusion, pred[16,4,128]{2,1,0:T(4,128)(4,1)S(1)} %iota_compare_fusion.5, bf16[16,512,256]{2,1,0:T(8,128)(2,1)} %param.12, ...), kind=kOutput, calls=%fused_computation.14 | convolution fusion | flops 2174738432 | bytes 25305152 | tf_op jit(solution)/shard_map/kuh,kech->keuc/dot_general | solution.py:56
  194.3 5.7 %copy-done.1 = f32[16,4,128,512]{3,2,1,0:T(8,128)} copy-done((f32[16,4,128,512]{3,2,1,0:T(8,128)}, f32[16,4,128,512]{3,2,1,0:T(8,128)S(1)}, u32[]{:S(2)}) %copy-start.1) | copy-done | bytes 16777240
  200.0 8.0 %fusion.2 = f32[16,4,128]{2,1,0:T(4,128)S(1)} fusion(f32[16,4,128,512]{3,2,1,0:T(8,128)S(1)} %get-tuple-element.9, f32[16,512]{1,0:T(8,128)S(1)} %broadcast_add_fusion.1, f32[16,4,128]{2,1,0:T(4,128)S(1)} %bitcast.74, f32[16,4,128]{2,1,0:T(4,128)S(1)} %bitcast.67, f32[16,512]{1,0:T(8,128)S(1)} %rsqrt_multiply_fusion, ...), kind=kLoop, calls=%fused_computation.20 | loop fusion | flops 33546240 | bytes 16957440 | tf_op jit(solution)/shard_map/reduce_sum | solution.py:89
  208.0 0.2 convolution_convert_fusion.3
  208.3 0.6 copy.94
  208.9 14.8 %all-to-all-start.4 = ((bf16[64,2,128]{2,1,0:T(2,128)(2,1)}), bf16[64,2,128]{2,1,0:T(2,128)(2,1)S(1)}, u32[]{:S(2)}, u32[]{:S(2)}) async-start(bf16[64,2,128]{2,1,0:T(2,128)(2,1)} %copy.94), calls=%async_computation.4 | async-start | bytes 65536 | tf_op jit(solution)/shard_map/all_to_all | solution.py:96
  223.7 0.5 broadcast.281
  224.2 0.7 reduce.6
  225.0 0.1 eq.74
  225.1 6.9 %all-to-all-done.4 = bf16[64,2,128]{2,1,0:T(2,128)(2,1)S(1)} async-done(((bf16[64,2,128]{2,1,0:T(2,128)(2,1)}), bf16[64,2,128]{2,1,0:T(2,128)(2,1)S(1)}, u32[]{:S(2)}, u32[]{:S(2)}) %all-to-all-start.4) | async-done | bytes 32800 | tf_op jit(solution)/shard_map/all_to_all | solution.py:96
  232.1 0.1 convolution_convert_fusion.2
  232.2 5.6 %psum.14 = bf16[128,128]{1,0:T(8,128)(2,1)S(1)} all-reduce(bf16[128,128]{1,0:T(8,128)(2,1)S(1)} %convolution_convert_fusion.2), channel_id=1, replica_groups=mesh['shard'=64,'rep'=2] {'rep'}, use_global_device_ids=true, to_apply=%region_7.10 | all-reduce | flops 16384 | bytes 65536 | tf_op jit(solution)/shard_map/psum | solution.py:102
  237.8 0.7 gather_fusion.6
  238.5 0.1 select_convert_fusion.1
  238.6 12.9 %all_to_all.52 = bf16[64,2,128]{2,1,0:T(2,128)(2,1)S(1)} all-to-all(bf16[64,2,128]{2,1,0:T(2,128)(2,1)S(1)} %select_convert_fusion.1), channel_id=1, replica_groups=mesh['shard'=64,'rep'=2] {'shard'}, dimensions={0} | all-to-all | bytes 65536 | tf_op jit(solution)/shard_map/all_to_all | solution.py:76
  251.5 0.6 gather_fusion.7
  252.2 8.2 %bitcast_reduce_fusion = f32[16,512]{1,0:T(8,128)S(1)} fusion(f32[16,4,128,512]{3,2,1,0:T(8,128)} %copy-done.1, f32[16,4,128]{2,1,0:T(4,128)S(1)} %bitcast.71, f32[16,4,128]{2,1,0:T(4,128)S(1)} %bitcast.68, f32[16,512]{1,0:T(8,128)S(1)} %rsqrt_multiply_fusion, pred[16,4,128]{2,1,0:T(4,128)(4,1)S(1)} %iota_compare_fusion.5), kind=kLoop, calls=%fused_computation.11 | loop fusion | flops 25157632 | bytes 16916480 | tf_op jit(solution)/shard_map/reduce_sum | solution.py:71
  260.4 2.4 copy-done.2
  262.8 8.0 %fusion.3 = f32[16,4,128]{2,1,0:T(4,128)S(1)} fusion(f32[16,4,128,512]{3,2,1,0:T(8,128)S(1)} %copy-done.2, f32[16,512]{1,0:T(8,128)S(1)} %broadcast_add_fusion, f32[16,4,128]{2,1,0:T(4,128)S(1)} %bitcast.72, f32[16,4,128]{2,1,0:T(4,128)S(1)} %bitcast.69, f32[16,512]{1,0:T(8,128)S(1)} %rsqrt_multiply_fusion, pred[16,4,128]{2,1,0:T(4,128)(4,1)S(1)} %iota_compare_fusion.5, ...), kind=kLoop, calls=%fused_computation.21 | loop fusion | flops 33546240 | bytes 16957440 | tf_op jit(solution)/shard_map/reduce_sum | solution.py:89
  270.9 0.2 convolution_convert_fusion.1
  271.2 12.9 %all_to_all.53 = bf16[64,2,128]{2,1,0:T(2,128)(2,1)S(1)} all-to-all(bf16[64,2,128]{2,1,0:T(2,128)(2,1)S(1)} %copy.97), channel_id=1, replica_groups=mesh['shard'=64,'rep'=2] {'shard'}, dimensions={0} | all-to-all | bytes 65536 | tf_op jit(solution)/shard_map/all_to_all | solution.py:96
  284.0 0.1 convolution_convert_fusion
  284.2 6.3 %psum.15 = bf16[128,128]{1,0:T(8,128)(2,1)S(1)} all-reduce(bf16[128,128]{1,0:T(8,128)(2,1)S(1)} %convolution_convert_fusion), channel_id=1, replica_groups=mesh['shard'=64,'rep'=2] {'rep'}, use_global_device_ids=true, to_apply=%region_10.13 | all-reduce | flops 16384 | bytes 65536 | tf_op jit(solution)/shard_map/psum | solution.py:102
  290.5 0.7 gather_fusion.8
  291.1 0.1 select_convert_fusion
  291.3 12.9 %all_to_all.54 = bf16[64,2,128]{2,1,0:T(2,128)(2,1)S(1)} all-to-all(bf16[64,2,128]{2,1,0:T(2,128)(2,1)S(1)} %select_convert_fusion), channel_id=1, replica_groups=mesh['shard'=64,'rep'=2] {'shard'}, dimensions={0} | all-to-all | bytes 65536 | tf_op jit(solution)/shard_map/all_to_all | solution.py:76
  304.2 0.6 gather_fusion.9
  304.8 7.7 %select_reduce_fusion = f32[16,512]{1,0:T(8,128)S(1)} fusion(f32[16,4,128,512]{3,2,1,0:T(8,128)} %copy-done.1, f32[16,4,128]{2,1,0:T(4,128)S(1)} %bitcast.75, f32[16,4,128]{2,1,0:T(4,128)S(1)} %bitcast.70, f32[16,512]{1,0:T(8,128)S(1)} %rsqrt_multiply_fusion, pred[16,4,128]{2,1,0:T(4,128)(4,1)S(1)} %iota_compare_fusion.5), kind=kLoop, calls=%fused_computation.16 | loop fusion | flops 25157632 | bytes 16916480 | tf_op jit(solution)/shard_map/reduce_sum | solution.py:71
  312.6 0.7 multiply_select_fusion
  (47 shorter events, 1.0 us)
Async XLA Ops:
  0.6 23.2 %copy-start = (s32[128]{0:T(128)S(1)}, s32[128]{0:T(128)}, u32[]{:S(2)}) copy-start(s32[128]{0:T(128)} %param.17) | copy-start | bytes 1540
  23.9 6.9 %copy-start.3 = (f32[128,128]{1,0:T(8,128)S(1)}, f32[128,128]{1,0:T(8,128)}, u32[]{:S(2)}) copy-start(f32[128,128]{1,0:T(8,128)} %param.18) | copy-start | bytes 196612
  26.1 15.9 %all-to-all-start.1 = ((bf16[64,1,2]{2,1,0:T(2,128)(2,1)}), bf16[64,1,2]{2,1,0:T(2,128)(2,1)S(1)}, u32[]{:S(2)}, u32[]{:S(2)}) async-start(bf16[64,1,2]{2,1,0:T(2,128)(2,1)} %copy.88), calls=%async_computation.1 | async-start | bytes 65536 | tf_op jit(solution)/shard_map/all_to_all | solution.py:39
  42.0 18.1 %all-to-all-start.3 = ((bf16[64,2,128]{2,1,0:T(2,128)(2,1)}), bf16[64,2,128]{2,1,0:T(2,128)(2,1)S(1)}, u32[]{:S(2)}, u32[]{:S(2)}) async-start(bf16[64,2,128]{2,1,0:T(2,128)(2,1)} %select_convert_fusion.2), calls=%async_computation.3 | async-start | bytes 65536 | tf_op jit(solution)/shard_map/all_to_all | solution.py:76
  51.8 17.9 %copy-start.6 = (s32[16]{0:T(128)S(1)}, s32[16]{0:T(128)}, u32[]{:S(2)}) copy-start(s32[16]{0:T(128)} %param.15) | copy-start | bytes 196
  60.1 115.4 %all-to-all-start.2 = ((bf16[64,2,128,256]{3,2,1,0:T(8,128)(2,1)}), bf16[64,2,128,256]{3,2,1,0:T(8,128)(2,1)}, u32[]{:S(2)}, u32[]{:S(2)}) async-start(bf16[64,2,128,256]{3,2,1,0:T(8,128)(2,1)} %broadcast_select_fusion), calls=%async_computation.2 | async-start | bytes 16777216 | tf_op jit(solution)/shard_map/all_to_all | solution.py:38
  194.3 5.7 %copy-start.1 = (f32[16,4,128,512]{3,2,1,0:T(8,128)}, f32[16,4,128,512]{3,2,1,0:T(8,128)S(1)}, u32[]{:S(2)}) copy-start(f32[16,4,128,512]{3,2,1,0:T(8,128)S(1)} %get-tuple-element.9) | copy-start | bytes 50331652
  194.3 43.5 %copy-start.5 = (f32[128,128]{1,0:T(8,128)S(1)}, f32[128,128]{1,0:T(8,128)}, u32[]{:S(2)}) copy-start(f32[128,128]{1,0:T(8,128)} %param.19) | copy-start | bytes 196612
  208.9 23.1 %all-to-all-start.4 = ((bf16[64,2,128]{2,1,0:T(2,128)(2,1)}), bf16[64,2,128]{2,1,0:T(2,128)(2,1)S(1)}, u32[]{:S(2)}, u32[]{:S(2)}) async-start(bf16[64,2,128]{2,1,0:T(2,128)(2,1)} %copy.94), calls=%async_computation.4 | async-start | bytes 65536 | tf_op jit(solution)/shard_map/all_to_all | solution.py:96
  252.1 10.7 %copy-start.2 = (f32[16,4,128,512]{3,2,1,0:T(8,128)S(1)}, f32[16,4,128,512]{3,2,1,0:T(8,128)}, u32[]{:S(2)}) copy-start(f32[16,4,128,512]{3,2,1,0:T(8,128)} %copy-done.1) | copy-start | bytes 50331652
  290.5 22.8 %copy-start.4 = (f32[128,128]{1,0:T(8,128)}, f32[128,128]{1,0:T(8,128)S(1)}, u32[]{:S(2)}) copy-start(f32[128,128]{1,0:T(8,128)S(1)} %add_maximum_fusion) | copy-start | bytes 196612
where the time goes:
time: 314 us; the launch traced here: 313 us
  waiting for transfers between devices  108 us (34%)
  blocking collectives  70.7 us (23%)
  other arithmetic  49.9 us (16%)
  starting transfers between devices  38.6 us (12%)
  local copies, waits for them, and re-layouts  35 us (11%)
  matrix products  9.89 us (3%)
    all_to_all x1, waiting for transfers between devices, body(): lax.all_to_all(reply_rows, 'shard', split_axis=0, concat_axis=0, tiled=True)  100 us
    all_to_all x2, blocking collectives, fetch_duals(): lax.all_to_all(outgoing.astype(jnp.bfloat16), 'shard', split_axis=0, conc...  25.8 us
    all_to_all x1, blocking collectives, body(): lax.all_to_all(wanted, 'shard', split_axis=0, concat_axis=0, tiled=True)  20.2 us
    reduce_sum x2, other arithmetic, new_duals(): jnp.sum(jnp.where(live_users[:, None, :, None], alloc_share, 0.0), axis=2)  16.1 us
    reduce_sum x2, other arithmetic, allocate(): denominator = 1.0 + jnp.sum(weights, axis=(1, 3))  16 us
    all_to_all x1, starting transfers between devices, new_duals(): lax.all_to_all(spend_slots.astype(jnp.bfloat16), 'shard', split_axis=0, c...  14.8 us
    all_to_all x1, blocking collectives, new_duals(): lax.all_to_all(spend_slots.astype(jnp.bfloat16), 'shard', split_axis=0, c...  12.9 us
    psum x2, blocking collectives, new_duals(): lax.psum(own_spend.astype(jnp.bfloat16), 'rep').astype(jnp.float32)  11.8 us
  transfers between devices with their start and end apart: 4, of which 3 were waited for; matrix products, arithmetic and copies ran while one was open for 8% of the time, Pallas kernels for 0%

commit v1 on v0

v1 whole, which is shorter than its diff:
```python
import functools
import math

import jax
import jax.numpy as jnp
from jax import lax
from jax.experimental import pallas as pl
from jax.experimental.pallas import tpu as pltpu
from jax.sharding import PartitionSpec as P

epsilon = 1e-06
temper = 0.25
sharpness = 16.0
HIGH = lax.Precision.HIGHEST
MESH = pl.DeviceIdType.MESH


def shift_digits(a, b, radix, sign):
    out = 0
    for place in (1, radix, radix * radix):
        digit = ((a // place) % radix + sign * ((b // place) % radix) + radix) % radix
        out = out + digit * place
    return out


def kernel(
    radix,
    item_slot,
    wanted,
    sizes,
    counts,
    dual_init,
    limits,
    to_slots,
    to_items,
    camp_hbm,
    user_hbm,
    user_out,
    dual_out,
    camps,
    users,
    user_scale,
    sendbuf,
    recvbuf,
    kmat,
    ids_in,
    ids_smem,
    row_send,
    row_recv,
    den_send,
    den_recv,
    dual_send,
    dual_recv,
    hit,
    hit_t,
    lam,
    vdup,
    camp_sem,
    user_sem,
    smem_sem,
    user_ssem,
    user_rsem,
    ids_ssem,
    ids_rsem,
    bulk_ssem,
    bulk_rsem,
    row_ssem,
    row_rsem,
    den_ssem,
    den_rsem,
    dual_ssem,
    dual_rsem,
):
    me = lax.axis_index("shard")
    rep = lax.axis_index("rep")
    n = wanted.shape[0]
    clusters, half_users, width = user_hbm.shape
    all_users = 2 * half_users
    half = camps.shape[1]
    lanes = 2 * half
    blocks = camps.shape[0]

    my_rows = pl.ds(pl.multiple_of(rep * half, half), half)
    my_users = pl.ds(pl.multiple_of(rep * half_users, half_users), half_users)
    load_camps = pltpu.make_async_copy(camp_hbm.at[:, my_rows, :], camps, camp_sem)
    load_camps.start()
    load_users = pltpu.make_async_copy(user_hbm, users.at[:, my_users, :], user_sem)
    load_users.start()

    barrier = pltpu.get_barrier_semaphore()

    @pl.loop(1, n)
    def _(d):
        pl.semaphore_signal(
            barrier, inc=1, device_id=(shift_digits(me, d, radix, 1), rep), device_id_type=MESH
        )

    pl.semaphore_signal(barrier, inc=1, device_id=(me, 1 - rep), device_id_type=MESH)
    pl.semaphore_wait(barrier, n)

    def remote(src, dst, ssem, rsem, target):
        return pltpu.make_async_remote_copy(
            src_ref=src, dst_ref=dst, send_sem=ssem, recv_sem=rsem,
            device_id=target, device_id_type=MESH,
        )

    def scatter(src, dst, ssem, rsem, sign):
        @pl.loop(1, n)
        def _(d):
            remote(
                src.at[d], dst.at[d], ssem, rsem, (shift_digits(me, d, radix, sign), rep)
            ).start()

    def all_of(src, dst, ssem, rsem):
        rest = pl.ds(1, n - 1)
        return remote(src.at[rest], dst.at[rest], ssem, rsem, (me, 1 - rep))

    scatter(wanted, ids_in, ids_ssem, ids_rsem, -1)
    swap_users = remote(
        user_hbm, users.at[:, my_users, :], user_ssem, user_rsem, (me, 1 - rep)
    )
    swap_users.start()
    ids_in[0] = wanted[0]

    lane = lax.broadcasted_iota(jnp.int32, (1, lanes), 1)
    left = lane < half

    def spread(x):
        rolled = pltpu.roll(x, half, 1)
        mine = left == (rep == 0)
        return jnp.where(mine, x, rolled)

    lam[...] = spread(dual_init[...])
    limit = spread(limits[...])
    live_camps = (lane % half) + rep * half < counts[...]

    def weights_of(duals):
        return jnp.where(live_camps, jnp.exp(duals * (-1.0 / temper)), 0.0)

    vdup[...] = weights_of(lam[...])

    all_of(wanted, ids_in, ids_ssem, ids_rsem).wait()
    to_smem = pltpu.make_async_copy(ids_in, ids_smem, smem_sem)
    to_smem.start()
    ids = ids_in[:, 0, :]
    block_ids = lax.broadcasted_iota(jnp.int32, (n, blocks), 1)
    hit[:n] = (jnp.broadcast_to(ids[:, 0:1], (n, blocks)) == block_ids).astype(jnp.float32)
    hit[n:] = (jnp.broadcast_to(ids[:, 1:2], (n, blocks)) == block_ids).astype(jnp.float32)

    def send_weights(step):
        picked = jnp.dot(hit[...], vdup[...], precision=HIGH, preferred_element_type=jnp.float32)
        row_send[step, :, 0, :] = jnp.where(left, picked[:n], picked[n:])
        scatter(row_send.at[step], row_recv.at[step], row_ssem.at[step], row_rsem.at[step], 1)
        row_recv[step, 0] = row_send[step, 0]

    def wait_rows(step):
        all_of(
            row_send.at[step], row_recv.at[step], row_ssem.at[step], row_rsem.at[step]
        ).wait()
        return row_recv[step, :, 0, :]

    send_weights(0)
    to_smem.wait()
    load_camps.wait()

    @pl.loop(1, n)
    def _(d):
        for j in range(2):
            sendbuf[2 * d + j] = camps[ids_smem[d, 0, j]]
        pair = pl.ds(2 * d, 2)
        remote(
            sendbuf.at[pair], recvbuf.at[pair], bulk_ssem, bulk_rsem,
            (shift_digits(me, d, radix, 1), rep),
        ).start()

    for j in range(2):
        recvbuf[j] = camps[ids_smem[0, 0, j]]

    hit_t[...] = hit[...].T
    load_users.wait()
    swap_users.wait()

    chunk = 256 if all_users % 256 == 0 else all_users
    chunks = all_users // chunk

    @pl.loop(0, clusters * chunks)
    def _(i):
        k = i // chunks
        at = pl.ds(pl.multiple_of((i % chunks) * chunk, chunk), chunk)
        x = users[k, at, :].astype(jnp.float32)
        mean = jnp.sum(x * x, axis=1, keepdims=True) * (1.0 / width)
        user_scale[k, at, :] = jnp.broadcast_to(lax.rsqrt(mean + epsilon), (chunk, 128))

    rest = pl.ds(2, 2 * n - 2)
    remote(sendbuf.at[rest], recvbuf.at[rest], bulk_ssem, bulk_rsem, (me, 1 - rep)).wait()

    factor = sharpness / width / temper * math.log2(math.e)
    fan = item_slot.shape[0] // clusters
    cols = fan * half

    @pl.loop(0, clusters)
    def _(k):
        emb = jnp.concatenate([recvbuf[item_slot[k * fan + e]] for e in range(fan)], axis=0)
        wide = emb.astype(jnp.float32)
        square = wide * wide
        upper = square.astype(jnp.bfloat16)
        lower = (square - upper.astype(jnp.float32)).astype(jnp.bfloat16)
        ones = jnp.ones((16, width), jnp.bfloat16)
        dims = (((1,), (1,)), ((), ()))
        total = lax.dot_general(ones, upper, dims, preferred_element_type=jnp.float32)
        total = total + lax.dot_general(ones, lower, dims, preferred_element_type=jnp.float32)
        camp_scale = lax.rsqrt(total[0:1] * (1.0 / width) + epsilon) * factor
        for c in range(chunks):
            at = pl.ds(c * chunk, chunk)
            raw = lax.dot_general(users[k, at, :], emb, dims, preferred_element_type=jnp.float32)
            scale = user_scale[k, at, :]
            wide_scale = jnp.concatenate([scale] * (cols // 128), axis=1)
            kmat[k, at, :] = jnp.exp2(raw * wide_scale * camp_scale).astype(jnp.bfloat16)

    def split(x):
        upper = x.astype(jnp.bfloat16)
        lower = (x - upper.astype(jnp.float32)).astype(jnp.bfloat16)
        return jnp.concatenate([upper, lower], axis=0)

    row_id = lax.broadcasted_iota(jnp.int32, (clusters, 1), 0)

    def denominator(step, rows):
        rolled = pltpu.roll(rows, half, 1)
        zero = jnp.zeros_like(rows)
        stack = jnp.concatenate(
            [jnp.where(left, rows, zero), jnp.where(left, rolled, zero),
             jnp.where(left, zero, rows), jnp.where(left, zero, rolled)], axis=0)
        table = jnp.dot(to_items[...], stack, precision=HIGH, preferred_element_type=jnp.float32)
        v = split(jnp.concatenate(
            [table[p * clusters:(p + 1) * clusters] for p in range(fan // 2)], axis=1))

        def add(k, acc):
            out = lax.dot_general(
                v, kmat[k], (((1,), (1,)), ((), ())), preferred_element_type=jnp.float32)
            return acc + jnp.where(row_id == k, out[:clusters] + out[clusters:], 0.0)

        part = lax.fori_loop(0, clusters, add, jnp.zeros((clusters, all_users), jnp.float32))
        den_send[step] = part
        swap = remote(
            den_send.at[step], den_recv.at[step], den_ssem.at[step], den_rsem.at[step],
            (me, 1 - rep))
        swap.start()
        swap.wait()
        return 1.0 + (part + den_recv[step])

    live_users = lax.broadcasted_iota(jnp.int32, (clusters, all_users), 1) < sizes[...]

    def sweep(step, rows):
        den = denominator(step, rows)
        q = split(jnp.where(live_users, 1.0 / den, 0.0))

        def add(k, acc):
            out = jnp.dot(q, kmat[k], preferred_element_type=jnp.float32)
            return acc + jnp.where(row_id == k, out[:clusters] + out[clusters:], 0.0)

        sums = lax.fori_loop(0, clusters, add, jnp.zeros((clusters, cols), jnp.float32))
        table = jnp.concatenate(
            [sums[:, p * lanes:(p + 1) * lanes] for p in range(fan // 2)], axis=0)
        rolled = pltpu.roll(table, half, 1)
        zero = jnp.zeros_like(table)
        stack = jnp.concatenate(
            [jnp.where(left, table, zero), jnp.where(left, rolled, zero),
             jnp.where(left, zero, table), jnp.where(left, zero, rolled)], axis=0)
        out = jnp.dot(to_slots[...], stack, precision=HIGH, preferred_element_type=jnp.float32)
        at = 2 * step + 1
        row_send[at, :, 0, :] = out
        scatter(row_send.at[at], row_recv.at[at], row_ssem.at[at], row_rsem.at[at], -1)
        row_recv[at, 0] = row_send[at, 0]
        got = wait_rows(at)
        turned = pltpu.roll(got, half, 1)
        both = jnp.concatenate(
            [jnp.where(left, got, turned), jnp.where(left, turned, got)], axis=0)
        spend = vdup[...] * jnp.dot(
            hit_t[...], both, precision=HIGH, preferred_element_type=jnp.float32)
        duals = jnp.maximum(
            0.0, lam[...] + temper * jnp.log((spend + limit) / (2.0 * limit)))
        lam[...] = duals
        vdup[...] = weights_of(duals)
        send_weights(at + 1)

    sweep(0, wait_rows(0))
    sweep(1, wait_rows(2))
    dual_send[...] = lam[...]
    swap_duals = remote(dual_send, dual_recv, dual_ssem, dual_rsem, (me, 1 - rep))
    swap_duals.start()
    den = denominator(2, wait_rows(4))
    result = jnp.where(live_users, temper * jnp.log(den), 0.0)
    user_out[...] = jnp.where(rep == 0, result[:, :half_users], result[:, half_users:])
    swap_duals.wait()
    dual_out[...] = jnp.where(left == (rep == 0), dual_send[...], dual_recv[...])


def body(
    user_emb, elig_owner, elig_local, cluster_size, camp_emb, camp_count, dual_init, spend_limit
):
    n = lax.axis_size("shard")
    radix = round(n ** (1 / 3))
    clusters, user_slots, width = user_emb.shape
    blocks, block_camps, _ = camp_emb.shape
    fan = elig_owner.shape[1]
    half = block_camps // 2
    me = lax.axis_index("shard")

    owners = elig_owner.reshape(-1)
    local_ids = elig_local.reshape(-1)
    items = owners.shape[0]
    earlier = jnp.arange(items)[None, :] < jnp.arange(items)[:, None]
    rank = jnp.sum(((owners[:, None] == owners[None, :]) & earlier).astype(jnp.int32), axis=1)
    dist = shift_digits(me, owners, radix, -1)
    item_slot = dist * 2 + rank

    slot_ids = jnp.arange(2 * n, dtype=jnp.int32)
    one_hot = item_slot[:, None] == slot_ids[None, :]
    wanted = jnp.sum(jnp.where(one_hot, local_ids[:, None], 0), axis=0).reshape(n, 2)
    first = jnp.arange(128)[None, None, :] == 0
    wanted = jnp.where(first, wanted[:, 0][:, None, None], wanted[:, 1][:, None, None])

    order = one_hot.astype(jnp.float32).reshape(clusters, fan // 2, 2, n, 2)
    order = order.transpose(1, 0, 2, 3, 4).reshape(clusters * fan // 2, 2, n, 2)
    even0, odd0 = order[:, 0, :, 0], order[:, 1, :, 0]
    even1, odd1 = order[:, 0, :, 1], order[:, 1, :, 1]
    to_slots = jnp.concatenate([even0, odd0, odd1, even1], axis=0).T
    to_items = jnp.concatenate([even0, even1, odd1, odd0], axis=1)

    vmem = pl.BlockSpec(memory_space=pltpu.VMEM)
    smem = pl.BlockSpec(memory_space=pltpu.SMEM)
    hbm = pl.BlockSpec(memory_space=pl.ANY)
    bf, f32, i32 = jnp.bfloat16, jnp.float32, jnp.int32
    dma = pltpu.SemaphoreType.DMA
    all_users = 2 * user_slots
    return pl.pallas_call(
        functools.partial(kernel, radix),
        out_shape=(
            jax.ShapeDtypeStruct((clusters, user_slots), f32),
            jax.ShapeDtypeStruct((blocks, block_camps), f32),
        ),
        in_specs=[smem] + [vmem] * 7 + [hbm] * 2,
        out_specs=(vmem, vmem),
        scratch_shapes=[
            pltpu.VMEM((blocks, half, width), bf),
            pltpu.VMEM((clusters, all_users, width), bf),
            pltpu.VMEM((clusters, all_users, 128), f32),
            pltpu.VMEM((2 * n, half, width), bf),
            pltpu.VMEM((2 * n, half, width), bf),
            pltpu.VMEM((clusters, all_users, fan * half), bf),
            pltpu.VMEM((n, 1, 128), i32),
            pltpu.SMEM((n, 1, 128), i32),
            pltpu.VMEM((5, n, 1, block_camps), f32),
            pltpu.VMEM((5, n, 1, block_camps), f32),
            pltpu.VMEM((3, clusters, all_users), f32),
            pltpu.VMEM((3, clusters, all_users), f32),
            pltpu.VMEM((blocks, block_camps), f32),
            pltpu.VMEM((blocks, block_camps), f32),
            pltpu.VMEM((2 * n, blocks), f32),
            pltpu.VMEM((blocks, 2 * n), f32),
            pltpu.VMEM((blocks, block_camps), f32),
            pltpu.VMEM((blocks, block_camps), f32),
            dma, dma, dma, dma, dma, dma, dma, dma, dma,
            dma((5,)), dma((5,)), dma((3,)), dma((3,)), dma, dma,
        ],
        compiler_params=pltpu.CompilerParams(
            collective_id=0, has_side_effects=True, vmem_limit_bytes=56 << 20
        ),
        name="allocate",
    )(
        item_slot, wanted, cluster_size.reshape(clusters, 1), camp_count.reshape(blocks, 1),
        dual_init, spend_limit, to_slots, to_items, camp_emb, user_emb,
    )


def solution(mesh):
    return jax.shard_map(
        body,
        mesh=mesh,
        in_specs=(
            P("shard", "rep", None),
            P("shard", None),
            P("shard", None),
            P("shard"),
            P("shard", None, None),
            P("shard"),
            P("shard", None),
            P("shard", None),
        ),
        out_specs=(P("shard", "rep"), P("shard", None)),
        check_vma=False,
    )
```

time: 314 us -> 163 us (0.52)
  Pallas kernels: 0 us -> 151 us
  waiting for transfers between devices: 108 us -> 0 us
  blocking collectives: 70.7 us -> 0 us
  other arithmetic: 49.9 us -> 2.65 us
  starting transfers between devices: 38.6 us -> 0 us
  local copies, waits for them, and re-layouts: 35 us -> 8.55 us
  matrix products: 9.89 us -> 0 us
    pallas_call x0 -> x1, Pallas kernels: none -> 151 us  [body(): pl.pallas_call(functools.partial(kernel, radix), out_shape=(jax.ShapeDtyp...]
    all_to_all x4 -> x0, waiting for transfers between devices: 108 us -> none  [the longest x1 100 us: body(): lax.all_to_all(reply_rows, 'shard', split_axis=0, concat_axis=0, tiled=True)]
    all_to_all x4 -> x0, blocking collectives: 58.8 us -> none  [the longest x2 25.8 us: fetch_duals(): lax.all_to_all(outgoing.astype(jnp.bfloat16), 'shard', split_axis=0, conc...]
    reduce_sum x8 -> x2, other arithmetic: 39.1 us -> 0.28 us  [the longest x1 0.18 us: body(): jnp.sum(((owners[:, None] == owners[None, :]) & earlier).astype(jnp.int32...]
    all_to_all x4 -> x0, starting transfers between devices: 38.6 us -> none  [the longest x1 14.8 us: new_duals(): lax.all_to_all(spend_slots.astype(jnp.bfloat16), 'shard', split_axis=0, c...]
    gather x13 -> x0, local copies, waits for them, and re-layouts: 22 us -> none  [the longest x1 9.78 us: body(): reply_rows = jnp.take(camp_emb, incoming, axis=0)]
    psum x2 -> x0, blocking collectives: 11.8 us -> none  [new_duals(): lax.psum(own_spend.astype(jnp.bfloat16), 'rep').astype(jnp.float32)]
    dot_general x5 -> x0, matrix products: 9.89 us -> none  [the longest x1 9.18 us: affinity(): jnp.einsum('kuh,kech->keuc', user_emb, item_emb, preferred_element_type=j...]
  transfers between devices with their start and end apart: 4 -> 0, of which waited for: 3 -> 0; matrix products, arithmetic and copies ran while one was open for 8% -> 0% of each run, Pallas kernels for 0% -> 0%
where the time goes in v1:
time: 163 us
  Pallas kernels  151 us (93%)
  local copies, waits for them, and re-layouts  8.55 us (5%)
  other arithmetic  2.65 us (2%)
    pallas_call x1, Pallas kernels, body(): pl.pallas_call(functools.partial(kernel, radix), out_shape=(jax.ShapeDtyp...  151 us
    unnamed x6, local copies, waits for them, and re-layouts  4.37 us

profile of v1, /device:TPU:1, one launch (start us, length us, event | category | flops | bytes accessed | tf_op | source)
XLA Modules:
  0.0 162.6 jit_solution(6255479684081333619)
XLA Ops:
  0.7 0.8 copy.25
  1.5 0.1 broadcast_in_dim.44
  1.6 1.3 copy.28.sizes
  2.9 0.8 copy.24
  3.7 0.1 reshape.260
  3.7 0.2 convert_reduce_fusion
  4.0 0.0 copy-start
  4.0 0.1 select_reduce_fusion
  4.1 0.1 reduce_sum.22
  4.2 0.1 copy.26
  4.3 0.7 add_bitcast_fusion
  5.0 0.1 eq.76
  5.1 0.1 reshape.261
  5.2 0.2 slice_reduce_fusion.1
  5.4 0.8 broadcast_select_fusion.wanted
  6.3 0.1 compare_convert_fusion
  6.3 0.7 pad_maximum_fusion.to_items
  7.0 0.7 copy.30.to_slots
  7.7 1.4 copy.29.counts
  9.1 0.0 copy-done
  9.1 150.6 %allocate.1 = (f32[16,512]{1,0:T(8,128)}, f32[128,128]{1,0:T(8,128)}) custom-call(s32[64]{0:T(128)} %copy-done, s32[64,1,128]{2,1,0:T(1,128)} %broadcast_select_fusion.wanted, s32[16,1]{1,0:T(8,128)} %copy.28.sizes, s32[128,1]{1,0:T(8,128)} %copy.29.counts, f32[128,128]{1,0:T(8,128)} %dual_init.1, f32[128,128]{1,0:T(8,128)} %limits.1, ...), custom_call_target="tpu_custom_call" | custom-call | tf_op jit(solution)/shard_map/allocate/pallas_call | solution.py:336
  159.7 1.4 copy.33
  161.1 1.5 copy.34
  (6 shorter events, 0.1 us)
Async XLA Ops:
  4.0 5.2 %copy-start = (s32[64]{0:T(128)}, s32[64]{0:T(128)S(1)}, u32[]{:S(2)}) copy-start(s32[64]{0:T(128)S(1)} %multiply_add_fusion.1.item_slot) | copy-start | bytes 772

commit v2 on v1

--- a/solution.py
+++ b/solution.py
@@ -11,28 +11,18 @@
 epsilon = 1e-06
 temper = 0.25
 sharpness = 16.0
-HIGH = lax.Precision.HIGHEST
+mix = 37
 MESH = pl.DeviceIdType.MESH
-
-
-def shift_digits(a, b, radix, sign):
-    out = 0
-    for place in (1, radix, radix * radix):
-        digit = ((a // place) % radix + sign * ((b // place) % radix) + radix) % radix
-        out = out + digit * place
-    return out
 
 
 def kernel(
     radix,
-    item_slot,
-    wanted,
-    sizes,
-    counts,
+    owner_ref,
+    local_ref,
+    size_ref,
+    count_ref,
     dual_init,
     limits,
-    to_slots,
-    to_items,
     camp_hbm,
     user_hbm,
     user_out,
@@ -43,8 +33,14 @@
     sendbuf,
     recvbuf,
     kmat,
+    rows_pad,
+    wanted,
+    slots,
+    slots_smem,
     ids_in,
     ids_smem,
+    to_slots,
+    to_items,
     row_send,
     row_recv,
     den_send,
@@ -58,6 +54,7 @@
     camp_sem,
     user_sem,
     smem_sem,
+    slot_sem,
     user_ssem,
     user_rsem,
     ids_ssem,
@@ -87,16 +84,27 @@
     load_users = pltpu.make_async_copy(user_hbm, users.at[:, my_users, :], user_sem)
     load_users.start()
 
+    places = (radix * radix, radix, 1)
+    digits = [(me // p) % radix for p in places]
+    moved = {
+        sign: [
+            [((digit + sign * j + radix) % radix) * p for j in range(radix)]
+            for digit, p in zip(digits, places)
+        ]
+        for sign in (1, -1)
+    }
+
+    def partner(d, sign):
+        return sum(moved[sign][i][(d // p) % radix] for i, p in enumerate(places))
+
+    order = [(i * mix) % n for i in range(1, n)]
+
     barrier = pltpu.get_barrier_semaphore()
-
-    @pl.loop(1, n)
-    def _(d):
+    for d in order:
         pl.semaphore_signal(
-            barrier, inc=1, device_id=(shift_digits(me, d, radix, 1), rep), device_id_type=MESH
+            barrier, inc=1, device_id=(partner(d, 1), rep), device_id_type=MESH
         )
-
     pl.semaphore_signal(barrier, inc=1, device_id=(me, 1 - rep), device_id_type=MESH)
-    pl.semaphore_wait(barrier, n)
 
     def remote(src, dst, ssem, rsem, target):
         return pltpu.make_async_remote_copy(
@@ -105,15 +113,58 @@
         )
 
     def scatter(src, dst, ssem, rsem, sign):
-        @pl.loop(1, n)
-        def _(d):
-            remote(
-                src.at[d], dst.at[d], ssem, rsem, (shift_digits(me, d, radix, sign), rep)
-            ).start()
+        for d in order:
+            remote(src.at[d], dst.at[d], ssem, rsem, (partner(d, sign), rep)).start()
 
     def all_of(src, dst, ssem, rsem):
         rest = pl.ds(1, n - 1)
         return remote(src.at[rest], dst.at[rest], ssem, rsem, (me, 1 - rep))
+
+    fan, _ = owner_ref.shape
+    i32, f32, bf16 = jnp.int32, jnp.float32, jnp.bfloat16
+    lane = lax.broadcasted_iota(i32, (1, lanes), 1)
+    left = lane < half
+    evens, odds = list(range(0, fan, 2)), list(range(1, fan, 2))
+    columns = evens + odds + odds + evens
+
+    def column_row(ref):
+        rows_pad[...] = jnp.zeros_like(rows_pad)
+        rows_pad[0:fan, 0:clusters] = ref[...]
+        row = rows_pad[...]
+        out = jnp.zeros((1, lanes), i32)
+        for at, e in enumerate(columns):
+            piece = row[e:e + 1]
+            out = out + (pltpu.roll(piece, at * clusters, 1) if at else piece)
+        return out
+
+    owner = column_row(owner_ref)
+    local = column_row(local_ref)
+    dist = jnp.zeros_like(owner)
+    shift = radix.bit_length() - 1
+    for i, p in enumerate(places):
+        digit = lax.shift_right_logical(owner, i32(p.bit_length() - 1)) & (radix - 1)
+        dist = dist + ((digits[i] - digit + radix) & (radix - 1)) * p
+    mask = dist == lax.broadcasted_iota(i32, (n, lanes), 0)
+    from_col = lax.broadcasted_iota(i32, (lanes, lanes), 0)
+    to_col = lax.broadcasted_iota(i32, (lanes, lanes), 1)
+    cluster_of = clusters - 1
+    ahead = (from_col < half) & ((from_col & cluster_of) < (to_col & cluster_of))
+    prefix = jnp.dot(
+        mask.astype(f32).astype(bf16), ahead.astype(f32).astype(bf16),
+        preferred_element_type=f32)
+    rank = (lane >= half).astype(i32)
+    chosen = mask & (prefix == rank.astype(f32))
+    to_slots[...] = chosen.astype(f32).astype(bf16)
+    to_items[...] = chosen.astype(f32).T.astype(bf16)
+    first = jnp.sum(jnp.where(chosen & left, local, 0), axis=1, keepdims=True)
+    second = jnp.sum(jnp.where(chosen & ~left, local, 0), axis=1, keepdims=True)
+    wanted[:, 0, :] = jnp.where(lane == 0, first, second)
+    slot = lax.broadcasted_iota(i32, (n, lanes), 0) * 2 + rank
+    slots[...] = jnp.sum(jnp.where(chosen, slot, 0), axis=0, keepdims=True)
+    slots_to_smem = pltpu.make_async_copy(slots, slots_smem, slot_sem)
+    slots_to_smem.start()
+
+    pl.semaphore_wait(barrier, n)
 
     scatter(wanted, ids_in, ids_ssem, ids_rsem, -1)
     swap_users = remote(
@@ -122,9 +173,6 @@
     swap_users.start()
     ids_in[0] = wanted[0]
 
-    lane = lax.broadcasted_iota(jnp.int32, (1, lanes), 1)
-    left = lane < half
-
     def spread(x):
         rolled = pltpu.roll(x, half, 1)
         mine = left == (rep == 0)
@@ -132,7 +180,14 @@
 
     lam[...] = spread(dual_init[...])
     limit = spread(limits[...])
-    live_camps = (lane % half) + rep * half < counts[...]
+    diagonal = from_col == to_col
+
+    def column(row):
+        return jnp.sum(jnp.where(diagonal[:blocks], row.astype(f32), 0.0), axis=1, keepdims=True)
+
+    counts = column(count_ref[...])
+    camp_pos = jnp.where(left, lane, lane - half) + rep * half
+    live_camps = camp_pos.astype(f32) < counts
 
     def weights_of(duals):
         return jnp.where(live_camps, jnp.exp(duals * (-1.0 / temper)), 0.0)
@@ -144,11 +199,21 @@
     to_smem.start()
     ids = ids_in[:, 0, :]
     block_ids = lax.broadcasted_iota(jnp.int32, (n, blocks), 1)
-    hit[:n] = (jnp.broadcast_to(ids[:, 0:1], (n, blocks)) == block_ids).astype(jnp.float32)
-    hit[n:] = (jnp.broadcast_to(ids[:, 1:2], (n, blocks)) == block_ids).astype(jnp.float32)
+    hits = jnp.concatenate(
+        [(jnp.broadcast_to(ids[:, j:j + 1], (n, blocks)) == block_ids).astype(f32)
+         for j in range(2)], axis=0)
+    hit[...] = hits.astype(bf16)
+    hit_t[...] = hits.T.astype(bf16)
+
+    def pick(table, x):
+        upper = x.astype(bf16)
+        lower = (x - upper.astype(f32)).astype(bf16)
+        out = jnp.dot(
+            table, jnp.concatenate([upper, lower], axis=1), preferred_element_type=f32)
+        return out[:, :lanes] + out[:, lanes:]
 
     def send_weights(step):
-        picked = jnp.dot(hit[...], vdup[...], precision=HIGH, preferred_element_type=jnp.float32)
+        picked = pick(hit[...], vdup[...])
         row_send[step, :, 0, :] = jnp.where(left, picked[:n], picked[n:])
         scatter(row_send.at[step], row_recv.at[step], row_ssem.at[step], row_rsem.at[step], 1)
         row_recv[step, 0] = row_send[step, 0]
@@ -159,24 +224,24 @@
         ).wait()
         return row_recv[step, :, 0, :]
 
-    send_weights(0)
     to_smem.wait()
     load_camps.wait()
 
-    @pl.loop(1, n)
-    def _(d):
+    def clamp(i, size):
+        return jnp.minimum(jnp.maximum(i, 0), size - 1)
+
+    for d in order:
         for j in range(2):
-            sendbuf[2 * d + j] = camps[ids_smem[d, 0, j]]
+            sendbuf[2 * d + j] = camps[clamp(ids_smem[d, 0, j], blocks)]
         pair = pl.ds(2 * d, 2)
         remote(
-            sendbuf.at[pair], recvbuf.at[pair], bulk_ssem, bulk_rsem,
-            (shift_digits(me, d, radix, 1), rep),
+            sendbuf.at[pair], recvbuf.at[pair], bulk_ssem, bulk_rsem, (partner(d, 1), rep)
         ).start()
 
     for j in range(2):
-        recvbuf[j] = camps[ids_smem[0, 0, j]]
-
-    hit_t[...] = hit[...].T
+        recvbuf[j] = camps[clamp(ids_smem[0, 0, j], blocks)]
+
+    send_weights(0)
     load_users.wait()
     swap_users.wait()
 
@@ -195,12 +260,18 @@
     remote(sendbuf.at[rest], recvbuf.at[rest], bulk_ssem, bulk_rsem, (me, 1 - rep)).wait()
 
     factor = sharpness / width / temper * math.log2(math.e)
-    fan = item_slot.shape[0] // clusters
     cols = fan * half
+
+    slots_to_smem.wait()
+    first_at = [columns.index(e) * clusters for e in range(fan)]
+    second_at = [(columns.index(e, fan)) * clusters for e in range(fan)]
 
     @pl.loop(0, clusters)
     def _(k):
-        emb = jnp.concatenate([recvbuf[item_slot[k * fan + e]] for e in range(fan)], axis=0)
+        emb = jnp.concatenate(
+            [recvbuf[clamp(
+                slots_smem[0, first_at[e] + k] + slots_smem[0, second_at[e] + k], 2 * n)]
+             for e in range(fan)], axis=0)
         wide = emb.astype(jnp.float32)
         square = wide * wide
         upper = square.astype(jnp.bfloat16)
@@ -224,13 +295,12 @@
 
     row_id = lax.broadcasted_iota(jnp.int32, (clusters, 1), 0)
 
+    part = fan * clusters // 2
+
     def denominator(step, rows):
-        rolled = pltpu.roll(rows, half, 1)
-        zero = jnp.zeros_like(rows)
-        stack = jnp.concatenate(
-            [jnp.where(left, rows, zero), jnp.where(left, rolled, zero),
-             jnp.where(left, zero, rows), jnp.where(left, zero, rolled)], axis=0)
-        table = jnp.dot(to_items[...], stack, precision=HIGH, preferred_element_type=jnp.float32)
+        picked = pick(to_items[...], rows)
+        a, b, c, d = [picked[p * part:(p + 1) * part] for p in range(4)]
+        table = jnp.where(left, a + pltpu.roll(d, half, 1), c + pltpu.roll(b, half, 1))
         v = split(jnp.concatenate(
             [table[p * clusters:(p + 1) * clusters] for p in range(fan // 2)], axis=1))
 
@@ -239,16 +309,19 @@
                 v, kmat[k], (((1,), (1,)), ((), ())), preferred_element_type=jnp.float32)
             return acc + jnp.where(row_id == k, out[:clusters] + out[clusters:], 0.0)
 
-        part = lax.fori_loop(0, clusters, add, jnp.zeros((clusters, all_users), jnp.float32))
-        den_send[step] = part
+        own = lax.fori_loop(0, clusters, add, jnp.zeros((clusters, all_users), f32))
+        den_send[step] = own
         swap = remote(
             den_send.at[step], den_recv.at[step], den_ssem.at[step], den_rsem.at[step],
             (me, 1 - rep))
         swap.start()
         swap.wait()
-        return 1.0 + (part + den_recv[step])
-
-    live_users = lax.broadcasted_iota(jnp.int32, (clusters, all_users), 1) < sizes[...]
+        return 1.0 + (own + den_recv[step])
+
+    sizes = jnp.sum(
+        jnp.where(diagonal[:clusters, :clusters], size_ref[...].astype(f32), 0.0),
+        axis=1, keepdims=True).astype(i32)
+    live_users = lax.broadcasted_iota(i32, (clusters, all_users), 1) < sizes
 
     def sweep(step, rows):
         den = denominator(step, rows)
@@ -266,7 +339,7 @@
         stack = jnp.concatenate(
             [jnp.where(left, table, zero), jnp.where(left, rolled, zero),
              jnp.where(left, zero, table), jnp.where(left, zero, rolled)], axis=0)
-        out = jnp.dot(to_slots[...], stack, precision=HIGH, preferred_element_type=jnp.float32)
+        out = pick(to_slots[...], stack)
         at = 2 * step + 1
         row_send[at, :, 0, :] = out
         scatter(row_send.at[at], row_recv.at[at], row_ssem.at[at], row_rsem.at[at], -1)
@@ -275,8 +348,7 @@
         turned = pltpu.roll(got, half, 1)
         both = jnp.concatenate(
             [jnp.where(left, got, turned), jnp.where(left, turned, got)], axis=0)
-        spend = vdup[...] * jnp.dot(
-            hit_t[...], both, precision=HIGH, preferred_element_type=jnp.float32)
+        spend = vdup[...] * pick(hit_t[...], both)
         duals = jnp.maximum(
             0.0, lam[...] + temper * jnp.log((spend + limit) / (2.0 * limit)))
         lam[...] = duals
@@ -304,31 +376,7 @@
     blocks, block_camps, _ = camp_emb.shape
     fan = elig_owner.shape[1]
     half = block_camps // 2
-    me = lax.axis_index("shard")
-
-    owners = elig_owner.reshape(-1)
-    local_ids = elig_local.reshape(-1)
-    items = owners.shape[0]
-    earlier = jnp.arange(items)[None, :] < jnp.arange(items)[:, None]
-    rank = jnp.sum(((owners[:, None] == owners[None, :]) & earlier).astype(jnp.int32), axis=1)
-    dist = shift_digits(me, owners, radix, -1)
-    item_slot = dist * 2 + rank
-
-    slot_ids = jnp.arange(2 * n, dtype=jnp.int32)
-    one_hot = item_slot[:, None] == slot_ids[None, :]
-    wanted = jnp.sum(jnp.where(one_hot, local_ids[:, None], 0), axis=0).reshape(n, 2)
-    first = jnp.arange(128)[None, None, :] == 0
-    wanted = jnp.where(first, wanted[:, 0][:, None, None], wanted[:, 1][:, None, None])
-
-    order = one_hot.astype(jnp.float32).reshape(clusters, fan // 2, 2, n, 2)
-    order = order.transpose(1, 0, 2, 3, 4).reshape(clusters * fan // 2, 2, n, 2)
-    even0, odd0 = order[:, 0, :, 0], order[:, 1, :, 0]
-    even1, odd1 = order[:, 0, :, 1], order[:, 1, :, 1]
-    to_slots = jnp.concatenate([even0, odd0, odd1, even1], axis=0).T
-    to_items = jnp.concatenate([even0, even1, odd1, odd0], axis=1)
-
     vmem = pl.BlockSpec(memory_space=pltpu.VMEM)
-    smem = pl.BlockSpec(memory_space=pltpu.SMEM)
     hbm = pl.BlockSpec(memory_space=pl.ANY)
     bf, f32, i32 = jnp.bfloat16, jnp.float32, jnp.int32
     dma = pltpu.SemaphoreType.DMA
@@ -339,7 +387,7 @@
             jax.ShapeDtypeStruct((clusters, user_slots), f32),
             jax.ShapeDtypeStruct((blocks, block_camps), f32),
         ),
-        in_specs=[smem] + [vmem] * 7 + [hbm] * 2,
+        in_specs=[vmem] * 6 + [hbm] * 2,
         out_specs=(vmem, vmem),
         scratch_shapes=[
             pltpu.VMEM((blocks, half, width), bf),
@@ -348,19 +396,25 @@
             pltpu.VMEM((2 * n, half, width), bf),
             pltpu.VMEM((2 * n, half, width), bf),
             pltpu.VMEM((clusters, all_users, fan * half), bf),
+            pltpu.VMEM((8, 128), i32),
+            pltpu.VMEM((n, 1, 128), i32),
+            pltpu.VMEM((1, 128), i32),
+            pltpu.SMEM((1, 128), i32),
             pltpu.VMEM((n, 1, 128), i32),
             pltpu.SMEM((n, 1, 128), i32),
+            pltpu.VMEM((n, 128), bf),
+            pltpu.VMEM((128, n), bf),
             pltpu.VMEM((5, n, 1, block_camps), f32),
             pltpu.VMEM((5, n, 1, block_camps), f32),
             pltpu.VMEM((3, clusters, all_users), f32),
             pltpu.VMEM((3, clusters, all_users), f32),
             pltpu.VMEM((blocks, block_camps), f32),
             pltpu.VMEM((blocks, block_camps), f32),
-            pltpu.VMEM((2 * n, blocks), f32),
-            pltpu.VMEM((blocks, 2 * n), f32),
+            pltpu.VMEM((2 * n, blocks), bf),
+            pltpu.VMEM((blocks, 2 * n), bf),
             pltpu.VMEM((blocks, block_camps), f32),
             pltpu.VMEM((blocks, block_camps), f32),
-            dma, dma, dma, dma, dma, dma, dma, dma, dma,
+            dma, dma, dma, dma, dma, dma, dma, dma, dma, dma,
             dma((5,)), dma((5,)), dma((3,)), dma((3,)), dma, dma,
         ],
         compiler_params=pltpu.CompilerParams(
@@ -368,8 +422,8 @@
         ),
         name="allocate",
     )(
-        item_slot, wanted, cluster_size.reshape(clusters, 1), camp_count.reshape(blocks, 1),
-        dual_init, spend_limit, to_slots, to_items, camp_emb, user_emb,
+        elig_owner.T, elig_local.T, cluster_size.reshape(1, clusters),
+        camp_count.reshape(1, blocks), dual_init, spend_limit, camp_emb, user_emb,
     )
 
 

time: 163 us -> 126 us (0.77)
  Pallas kernels: 151 us -> 122 us
  local copies, waits for them, and re-layouts: 8.55 us -> 2.85 us
  other arithmetic: 2.65 us -> 0 us
    pallas_call x1, Pallas kernels: 151 us -> 122 us  [body(): pl.pallas_call(functools.partial(kernel, radix), out_shape=(jax.ShapeDtyp...]
    reshape x4 -> x0, local copies, waits for them, and re-layouts: 2.93 us -> none  [the longest x1 1.39 us: body(): camp_count.reshape(blocks, 1)]
    unnamed x6 -> x2, local copies, waits for them, and re-layouts: 4.37 us -> 2.85 us
where the time goes in v2:
time: 126 us
  Pallas kernels  122 us (97%)
  local copies, waits for them, and re-layouts  2.85 us (2%)
    pallas_call x1, Pallas kernels, body(): pl.pallas_call(functools.partial(kernel, radix), out_shape=(jax.ShapeDtyp...  122 us
    unnamed x2, local copies, waits for them, and re-layouts  2.85 us

profile of v2, /device:TPU:1, one launch (start us, length us, event | category | flops | bytes accessed | tf_op | source)
XLA Modules:
  0.0 125.7 jit_solution(15237041745253534765)
XLA Ops:
  0.6 122.3 %allocate.1 = (f32[16,512]{1,0:T(8,128)}, f32[128,128]{1,0:T(8,128)}) custom-call(s32[4,16]{1,0:T(4,128)} %bitcast.4, s32[4,16]{1,0:T(4,128)} %bitcast.5, s32[1,16]{1,0:T(1,128)} %bitcast.6, s32[1,128]{1,0:T(1,128)} %bitcast.7, f32[128,128]{1,0:T(8,128)} %dual_init.1, f32[128,128]{1,0:T(8,128)} %limits.1, bf16[128,128,256]{2,1,0:T(8,128)(2,1)} %camp_hbm.1, ...), custom_call_target="tpu_custom_call" | custom-call | tf_op jit(solution)/shard_map/allocate/pallas_call | solution.py:384
  122.9 1.4 %copy.12 = f32[16,512]{1,0:T(8,128)} copy(f32[16,512]{1,0:T(8,128)} %get-tuple-element.4) | data formatting | bytes 65536
  124.3 1.5 %copy.13 = f32[128,128]{1,0:T(8,128)} copy(f32[128,128]{1,0:T(8,128)} %get-tuple-element.5) | data formatting | bytes 131072

commit v3 on v2

--- a/solution.py
+++ b/solution.py
@@ -45,6 +45,8 @@
     row_recv,
     den_send,
     den_recv,
+    last_send,
+    last_recv,
     dual_send,
     dual_recv,
     hit,
@@ -97,7 +99,18 @@
     def partner(d, sign):
         return sum(moved[sign][i][(d // p) % radix] for i, p in enumerate(places))
 
+    def hops(d):
+        steps = [(d // p) % radix for p in places]
+        return sum(min(t, radix - t) for t in steps)
+
     order = [(i * mix) % n for i in range(1, n)]
+
+    def hops(d):
+        steps = [(d // p) % radix for p in places]
+        return sum(min(t, radix - t) for t in steps)
+
+    bulk_order = sorted(order, key=lambda d: hops(d) <= 1)
+    order = sorted(order, key=lambda d: -hops(d))
 
     barrier = pltpu.get_barrier_semaphore()
     for d in order:
@@ -230,7 +243,7 @@
     def clamp(i, size):
         return jnp.minimum(jnp.maximum(i, 0), size - 1)
 
-    for d in order:
+    for d in bulk_order:
         for j in range(2):
             sendbuf[2 * d + j] = camps[clamp(ids_smem[d, 0, j], blocks)]
         pair = pl.ds(2 * d, 2)
@@ -266,7 +279,7 @@
     first_at = [columns.index(e) * clusters for e in range(fan)]
     second_at = [(columns.index(e, fan)) * clusters for e in range(fan)]
 
-    @pl.loop(0, clusters)
+    @pl.loop(0, clusters, unroll=4)
     def _(k):
         emb = jnp.concatenate(
             [recvbuf[clamp(
@@ -293,45 +306,60 @@
         lower = (x - upper.astype(jnp.float32)).astype(jnp.bfloat16)
         return jnp.concatenate([upper, lower], axis=0)
 
-    row_id = lax.broadcasted_iota(jnp.int32, (clusters, 1), 0)
-
     part = fan * clusters // 2
-
-    def denominator(step, rows):
-        picked = pick(to_items[...], rows)
-        a, b, c, d = [picked[p * part:(p + 1) * part] for p in range(4)]
-        table = jnp.where(left, a + pltpu.roll(d, half, 1), c + pltpu.roll(b, half, 1))
-        v = split(jnp.concatenate(
-            [table[p * clusters:(p + 1) * clusters] for p in range(fan // 2)], axis=1))
-
-        def add(k, acc):
-            out = lax.dot_general(
-                v, kmat[k], (((1,), (1,)), ((), ())), preferred_element_type=jnp.float32)
-            return acc + jnp.where(row_id == k, out[:clusters] + out[clusters:], 0.0)
-
-        own = lax.fori_loop(0, clusters, add, jnp.zeros((clusters, all_users), f32))
-        den_send[step] = own
-        swap = remote(
-            den_send.at[step], den_recv.at[step], den_ssem.at[step], den_rsem.at[step],
-            (me, 1 - rep))
-        swap.start()
-        swap.wait()
-        return 1.0 + (own + den_recv[step])
+    group = clusters // 2
+    row_id = lax.broadcasted_iota(i32, (group, 1), 0)
 
     sizes = jnp.sum(
         jnp.where(diagonal[:clusters, :clusters], size_ref[...].astype(f32), 0.0),
         axis=1, keepdims=True).astype(i32)
     live_users = lax.broadcasted_iota(i32, (clusters, all_users), 1) < sizes
 
+    def item_weights(rows):
+        picked = pick(to_items[...], rows)
+        a, b, c, d = [picked[p * part:(p + 1) * part] for p in range(4)]
+        table = jnp.where(left, a + pltpu.roll(d, half, 1), c + pltpu.roll(b, half, 1))
+        return split(jnp.concatenate(
+            [table[p * clusters:(p + 1) * clusters] for p in range(fan // 2)], axis=1))
+
+    def partial_sums(v, h):
+        at = h * group
+
+        def add(k, acc):
+            out = lax.dot_general(
+                v, kmat[k], (((1,), (1,)), ((), ())), preferred_element_type=f32)
+            both = out[at:at + group] + out[clusters + at:clusters + at + group]
+            return acc + jnp.where(row_id == k - at, both, 0.0)
+
+        zero = jnp.zeros((group, all_users), f32)
+        return lax.fori_loop(at, at + group, add, zero, unroll=4)
+
     def sweep(step, rows):
-        den = denominator(step, rows)
-        q = split(jnp.where(live_users, 1.0 / den, 0.0))
-
-        def add(k, acc):
-            out = jnp.dot(q, kmat[k], preferred_element_type=jnp.float32)
-            return acc + jnp.where(row_id == k, out[:clusters] + out[clusters:], 0.0)
-
-        sums = lax.fori_loop(0, clusters, add, jnp.zeros((clusters, cols), jnp.float32))
+        v = item_weights(rows)
+        own, swaps, sums = [], [], []
+        for h in range(2):
+            own.append(partial_sums(v, h))
+            at = pl.ds(h * group, group)
+            den_send[step, at] = own[h]
+            swaps.append(remote(
+                den_send.at[step, at], den_recv.at[step, at],
+                den_ssem.at[2 * step + h], den_rsem.at[2 * step + h], (me, 1 - rep)))
+            swaps[h].start()
+        for h in range(2):
+            at = h * group
+            swaps[h].wait()
+            den = 1.0 + (own[h] + den_recv[step, at:at + group])
+            q = jnp.where(live_users[at:at + group], 1.0 / den, 0.0)
+            upper = q.astype(bf16).astype(f32)
+            q = jnp.concatenate([upper, q - upper], axis=0).astype(bf16)
+
+            def add(k, acc, q=q, at=at):
+                out = jnp.dot(q, kmat[k], preferred_element_type=f32)
+                return acc + jnp.where(row_id == k - at, out[:group] + out[group:], 0.0)
+
+            sums.append(lax.fori_loop(
+                at, at + group, add, jnp.zeros((group, cols), f32), unroll=4))
+        sums = jnp.concatenate(sums, axis=0)
         table = jnp.concatenate(
             [sums[:, p * lanes:(p + 1) * lanes] for p in range(fan // 2)], axis=0)
         rolled = pltpu.roll(table, half, 1)
@@ -360,9 +388,25 @@
     dual_send[...] = lam[...]
     swap_duals = remote(dual_send, dual_recv, dual_ssem, dual_rsem, (me, 1 - rep))
     swap_duals.start()
-    den = denominator(2, wait_rows(4))
-    result = jnp.where(live_users, temper * jnp.log(den), 0.0)
-    user_out[...] = jnp.where(rep == 0, result[:, :half_users], result[:, half_users:])
+    v = item_weights(wait_rows(4))
+    mine, swaps = [], []
+    for h in range(2):
+        own = partial_sums(v, h)
+        low, high = own[:, :half_users], own[:, half_users:]
+        mine.append(jnp.where(rep == 0, low, high))
+        at = pl.ds(h * group, group)
+        last_send[at] = jnp.where(rep == 0, high, low)
+        swaps.append(remote(
+            last_send.at[at], last_recv.at[at], den_ssem.at[4 + h], den_rsem.at[4 + h],
+            (me, 1 - rep)))
+        swaps[h].start()
+    user_pos = lax.broadcasted_iota(i32, (clusters, half_users), 1) + rep * half_users
+    for h in range(2):
+        at = h * group
+        swaps[h].wait()
+        den = 1.0 + (mine[h] + last_recv[at:at + group])
+        user_out[at:at + group] = jnp.where(
+            user_pos[at:at + group] < sizes[at:at + group], temper * jnp.log(den), 0.0)
     swap_duals.wait()
     dual_out[...] = jnp.where(left == (rep == 0), dual_send[...], dual_recv[...])
 
@@ -406,8 +450,10 @@
             pltpu.VMEM((128, n), bf),
             pltpu.VMEM((5, n, 1, block_camps), f32),
             pltpu.VMEM((5, n, 1, block_camps), f32),
-            pltpu.VMEM((3, clusters, all_users), f32),
-            pltpu.VMEM((3, clusters, all_users), f32),
+            pltpu.VMEM((2, clusters, all_users), f32),
+            pltpu.VMEM((2, clusters, all_users), f32),
+            pltpu.VMEM((clusters, user_slots), f32),
+            pltpu.VMEM((clusters, user_slots), f32),
             pltpu.VMEM((blocks, block_camps), f32),
             pltpu.VMEM((blocks, block_camps), f32),
             pltpu.VMEM((2 * n, blocks), bf),
@@ -415,7 +461,7 @@
             pltpu.VMEM((blocks, block_camps), f32),
             pltpu.VMEM((blocks, block_camps), f32),
             dma, dma, dma, dma, dma, dma, dma, dma, dma, dma,
-            dma((5,)), dma((5,)), dma((3,)), dma((3,)), dma, dma,
+            dma((5,)), dma((5,)), dma((6,)), dma((6,)), dma, dma,
         ],
         compiler_params=pltpu.CompilerParams(
             collective_id=0, has_side_effects=True, vmem_limit_bytes=56 << 20

time: 126 us -> 113 us (0.90)
  Pallas kernels: 122 us -> 109 us
    pallas_call x1, Pallas kernels: 122 us -> 109 us  [body(): pl.pallas_call(functools.partial(kernel, radix), out_shape=(jax.ShapeDtyp...]
where the time goes in v3:
time: 113 us; the launch traced here: 112 us
  Pallas kernels  109 us (96%)
  local copies, waits for them, and re-layouts  2.85 us (3%)
    pallas_call x1, Pallas kernels, body(): pl.pallas_call(functools.partial(kernel, radix), out_shape=(jax.ShapeDtyp...  109 us
    unnamed x2, local copies, waits for them, and re-layouts  2.85 us

profile of v3, /device:TPU:1, one launch (start us, length us, event | category | flops | bytes accessed | tf_op | source)
XLA Modules:
  0.0 112.4 jit_solution(10905009015256883824)
XLA Ops:
  0.6 108.9 %allocate.1 = (f32[16,512]{1,0:T(8,128)}, f32[128,128]{1,0:T(8,128)}) custom-call(s32[4,16]{1,0:T(4,128)} %bitcast.4, s32[4,16]{1,0:T(4,128)} %bitcast.5, s32[1,16]{1,0:T(1,128)} %bitcast.6, s32[1,128]{1,0:T(1,128)} %bitcast.7, f32[128,128]{1,0:T(8,128)} %dual_init.1, f32[128,128]{1,0:T(8,128)} %limits.1, bf16[128,128,256]{2,1,0:T(8,128)(2,1)} %camp_hbm.1, ...), custom_call_target="tpu_custom_call" | custom-call | tf_op jit(solution)/shard_map/allocate/pallas_call | solution.py:428
  109.5 1.4 %copy.12 = f32[16,512]{1,0:T(8,128)} copy(f32[16,512]{1,0:T(8,128)} %get-tuple-element.4) | data formatting | bytes 65536
  110.9 1.5 %copy.13 = f32[128,128]{1,0:T(8,128)} copy(f32[128,128]{1,0:T(8,128)} %get-tuple-element.5) | data formatting | bytes 131072

commit v4 on v3

--- a/solution.py
+++ b/solution.py
@@ -17,14 +17,22 @@
 
 def kernel(
     radix,
+    owner_hbm,
+    local_hbm,
+    size_hbm,
+    count_hbm,
+    init_hbm,
+    limit_hbm,
+    camp_hbm,
+    user_hbm,
+    user_out_hbm,
+    dual_out_hbm,
     owner_ref,
     local_ref,
     size_ref,
     count_ref,
     dual_init,
     limits,
-    camp_hbm,
-    user_hbm,
     user_out,
     dual_out,
     camps,
@@ -53,6 +61,8 @@
     hit_t,
     lam,
     vdup,
+    small_sem,
+    out_sem,
     camp_sem,
     user_sem,
     smem_sem,
@@ -79,13 +89,6 @@
     lanes = 2 * half
     blocks = camps.shape[0]
 
-    my_rows = pl.ds(pl.multiple_of(rep * half, half), half)
-    my_users = pl.ds(pl.multiple_of(rep * half_users, half_users), half_users)
-    load_camps = pltpu.make_async_copy(camp_hbm.at[:, my_rows, :], camps, camp_sem)
-    load_camps.start()
-    load_users = pltpu.make_async_copy(user_hbm, users.at[:, my_users, :], user_sem)
-    load_users.start()
-
     places = (radix * radix, radix, 1)
     digits = [(me // p) % radix for p in places]
     moved = {
@@ -119,6 +122,24 @@
         )
     pl.semaphore_signal(barrier, inc=1, device_id=(me, 1 - rep), device_id_type=MESH)
 
+    def fetch(src, dst, i):
+        copy = pltpu.make_async_copy(src, dst, small_sem.at[i])
+        copy.start()
+        return copy
+
+    get_owner = fetch(owner_hbm, owner_ref, 0)
+    get_local = fetch(local_hbm, local_ref, 1)
+    get_rest = [
+        fetch(size_hbm, size_ref, 2), fetch(count_hbm, count_ref, 3),
+        fetch(init_hbm, dual_init, 4), fetch(limit_hbm, limits, 5),
+    ]
+    my_rows = pl.ds(pl.multiple_of(rep * half, half), half)
+    my_users = pl.ds(pl.multiple_of(rep * half_users, half_users), half_users)
+    load_camps = pltpu.make_async_copy(camp_hbm.at[:, my_rows, :], camps, camp_sem)
+    load_camps.start()
+    load_users = pltpu.make_async_copy(user_hbm, users.at[:, my_users, :], user_sem)
+    load_users.start()
+
     def remote(src, dst, ssem, rsem, target):
         return pltpu.make_async_remote_copy(
             src_ref=src, dst_ref=dst, send_sem=ssem, recv_sem=rsem,
@@ -150,6 +171,8 @@
             out = out + (pltpu.roll(piece, at * clusters, 1) if at else piece)
         return out
 
+    get_owner.wait()
+    get_local.wait()
     owner = column_row(owner_ref)
     local = column_row(local_ref)
     dist = jnp.zeros_like(owner)
@@ -191,6 +214,8 @@
         mine = left == (rep == 0)
         return jnp.where(mine, x, rolled)
 
+    for copy in get_rest:
+        copy.wait()
     lam[...] = spread(dual_init[...])
     limit = spread(limits[...])
     diagonal = from_col == to_col
@@ -332,7 +357,7 @@
             return acc + jnp.where(row_id == k - at, both, 0.0)
 
         zero = jnp.zeros((group, all_users), f32)
-        return lax.fori_loop(at, at + group, add, zero, unroll=4)
+        return lax.fori_loop(at, at + group, add, zero, unroll=8)
 
     def sweep(step, rows):
         v = item_weights(rows)
@@ -358,7 +383,7 @@
                 return acc + jnp.where(row_id == k - at, out[:group] + out[group:], 0.0)
 
             sums.append(lax.fori_loop(
-                at, at + group, add, jnp.zeros((group, cols), f32), unroll=4))
+                at, at + group, add, jnp.zeros((group, cols), f32), unroll=8))
         sums = jnp.concatenate(sums, axis=0)
         table = jnp.concatenate(
             [sums[:, p * lanes:(p + 1) * lanes] for p in range(fan // 2)], axis=0)
@@ -400,6 +425,10 @@
             last_send.at[at], last_recv.at[at], den_ssem.at[4 + h], den_rsem.at[4 + h],
             (me, 1 - rep)))
         swaps[h].start()
+    swap_duals.wait()
+    dual_out[...] = jnp.where(left == (rep == 0), dual_send[...], dual_recv[...])
+    put_duals = pltpu.make_async_copy(dual_out, dual_out_hbm, out_sem.at[0])
+    put_duals.start()
     user_pos = lax.broadcasted_iota(i32, (clusters, half_users), 1) + rep * half_users
     for h in range(2):
         at = h * group
@@ -407,8 +436,10 @@
         den = 1.0 + (mine[h] + last_recv[at:at + group])
         user_out[at:at + group] = jnp.where(
             user_pos[at:at + group] < sizes[at:at + group], temper * jnp.log(den), 0.0)
-    swap_duals.wait()
-    dual_out[...] = jnp.where(left == (rep == 0), dual_send[...], dual_recv[...])
+    put_users = pltpu.make_async_copy(user_out, user_out_hbm, out_sem.at[1])
+    put_users.start()
+    put_duals.wait()
+    put_users.wait()
 
 
 def body(
@@ -420,7 +451,6 @@
     blocks, block_camps, _ = camp_emb.shape
     fan = elig_owner.shape[1]
     half = block_camps // 2
-    vmem = pl.BlockSpec(memory_space=pltpu.VMEM)
     hbm = pl.BlockSpec(memory_space=pl.ANY)
     bf, f32, i32 = jnp.bfloat16, jnp.float32, jnp.int32
     dma = pltpu.SemaphoreType.DMA
@@ -431,9 +461,17 @@
             jax.ShapeDtypeStruct((clusters, user_slots), f32),
             jax.ShapeDtypeStruct((blocks, block_camps), f32),
         ),
-        in_specs=[vmem] * 6 + [hbm] * 2,
-        out_specs=(vmem, vmem),
+        in_specs=[hbm] * 8,
+        out_specs=(hbm, hbm),
         scratch_shapes=[
+            pltpu.VMEM((fan, clusters), i32),
+            pltpu.VMEM((fan, clusters), i32),
+            pltpu.VMEM((1, clusters), i32),
+            pltpu.VMEM((1, blocks), i32),
+            pltpu.VMEM((blocks, block_camps), f32),
+            pltpu.VMEM((blocks, block_camps), f32),
+            pltpu.VMEM((clusters, user_slots), f32),
+            pltpu.VMEM((blocks, block_camps), f32),
             pltpu.VMEM((blocks, half, width), bf),
             pltpu.VMEM((clusters, all_users, width), bf),
             pltpu.VMEM((clusters, all_users, 128), f32),
@@ -460,7 +498,7 @@
             pltpu.VMEM((blocks, 2 * n), bf),
             pltpu.VMEM((blocks, block_camps), f32),
             pltpu.VMEM((blocks, block_camps), f32),
-            dma, dma, dma, dma, dma, dma, dma, dma, dma, dma,
+            dma((6,)), dma((2,)), dma, dma, dma, dma, dma, dma, dma, dma, dma, dma,
             dma((5,)), dma((5,)), dma((6,)), dma((6,)), dma, dma,
         ],
         compiler_params=pltpu.CompilerParams(

time: 113 us -> 111 us (0.982)
  Pallas kernels: 109 us -> 107 us
    pallas_call x1, Pallas kernels: 109 us -> 107 us  [body(): pl.pallas_call(functools.partial(kernel, radix), out_shape=(jax.ShapeDtyp...]
where the time goes in v4:
time: 111 us
  Pallas kernels  107 us (96%)
  local copies, waits for them, and re-layouts  2.85 us (3%)
    pallas_call x1, Pallas kernels, body(): pl.pallas_call(functools.partial(kernel, radix), out_shape=(jax.ShapeDtyp...  107 us
    unnamed x2, local copies, waits for them, and re-layouts  2.85 us

profile of v4, /device:TPU:1, one launch (start us, length us, event | category | flops | bytes accessed | tf_op | source)
XLA Modules:
  0.0 110.7 jit_solution(15850927893944448583)
XLA Ops:
  0.6 107.2 %allocate.1 = (f32[16,512]{1,0:T(8,128)}, f32[128,128]{1,0:T(8,128)}) custom-call(s32[4,16]{1,0:T(4,128)} %bitcast.4, s32[4,16]{1,0:T(4,128)} %bitcast.5, s32[1,16]{1,0:T(1,128)} %bitcast.6, s32[1,128]{1,0:T(1,128)} %bitcast.7, f32[128,128]{1,0:T(8,128)} %init_hbm.1, f32[128,128]{1,0:T(8,128)} %limit_hbm.1, bf16[128,128,256]{2,1,0:T(8,128)(2,1)} %camp_hbm.1, ...), custom_call_target="tpu_custom_call" | custom-call | tf_op jit(solution)/shard_map/allocate/pallas_call | solution.py:458
  107.9 1.4 %copy.12 = f32[16,512]{1,0:T(8,128)} copy(f32[16,512]{1,0:T(8,128)} %get-tuple-element.4) | data formatting | bytes 65536
  109.2 1.5 %copy.13 = f32[128,128]{1,0:T(8,128)} copy(f32[128,128]{1,0:T(8,128)} %get-tuple-element.5) | data formatting | bytes 131072

commit v5 on v4

--- a/solution.py
+++ b/solution.py
@@ -235,6 +235,42 @@
     all_of(wanted, ids_in, ids_ssem, ids_rsem).wait()
     to_smem = pltpu.make_async_copy(ids_in, ids_smem, smem_sem)
     to_smem.start()
+    def pick(table, x):
+        upper = x.astype(bf16)
+        lower = (x - upper.astype(f32)).astype(bf16)
+        out = jnp.dot(
+            table, jnp.concatenate([upper, lower], axis=1), preferred_element_type=f32)
+        return out[:, :lanes] + out[:, lanes:]
+
+    def send_weights(step):
+        picked = pick(hit[...], vdup[...])
+        row_send[step, :, 0, :] = jnp.where(left, picked[:n], picked[n:])
+        scatter(row_send.at[step], row_recv.at[step], row_ssem.at[step], row_rsem.at[step], 1)
+        row_recv[step, 0] = row_send[step, 0]
+
+    def wait_rows(step):
+        all_of(
+            row_send.at[step], row_recv.at[step], row_ssem.at[step], row_rsem.at[step]
+        ).wait()
+        return row_recv[step, :, 0, :]
+
+    to_smem.wait()
+    load_camps.wait()
+
+    def clamp(i, size):
+        return jnp.minimum(jnp.maximum(i, 0), size - 1)
+
+    for d in bulk_order:
+        for j in range(2):
+            sendbuf[2 * d + j] = camps[clamp(ids_smem[d, 0, j], blocks)]
+        pair = pl.ds(2 * d, 2)
+        remote(
+            sendbuf.at[pair], recvbuf.at[pair], bulk_ssem, bulk_rsem, (partner(d, 1), rep)
+        ).start()
+
+    for j in range(2):
+        recvbuf[j] = camps[clamp(ids_smem[0, 0, j], blocks)]
+
     ids = ids_in[:, 0, :]
     block_ids = lax.broadcasted_iota(jnp.int32, (n, blocks), 1)
     hits = jnp.concatenate(
@@ -242,43 +278,6 @@
          for j in range(2)], axis=0)
     hit[...] = hits.astype(bf16)
     hit_t[...] = hits.T.astype(bf16)
-
-    def pick(table, x):
-        upper = x.astype(bf16)
-        lower = (x - upper.astype(f32)).astype(bf16)
-        out = jnp.dot(
-            table, jnp.concatenate([upper, lower], axis=1), preferred_element_type=f32)
-        return out[:, :lanes] + out[:, lanes:]
-
-    def send_weights(step):
-        picked = pick(hit[...], vdup[...])
-        row_send[step, :, 0, :] = jnp.where(left, picked[:n], picked[n:])
-        scatter(row_send.at[step], row_recv.at[step], row_ssem.at[step], row_rsem.at[step], 1)
-        row_recv[step, 0] = row_send[step, 0]
-
-    def wait_rows(step):
-        all_of(
-            row_send.at[step], row_recv.at[step], row_ssem.at[step], row_rsem.at[step]
-        ).wait()
-        return row_recv[step, :, 0, :]
-
-    to_smem.wait()
-    load_camps.wait()
-
-    def clamp(i, size):
-        return jnp.minimum(jnp.maximum(i, 0), size - 1)
-
-    for d in bulk_order:
-        for j in range(2):
-            sendbuf[2 * d + j] = camps[clamp(ids_smem[d, 0, j], blocks)]
-        pair = pl.ds(2 * d, 2)
-        remote(
-            sendbuf.at[pair], recvbuf.at[pair], bulk_ssem, bulk_rsem, (partner(d, 1), rep)
-        ).start()
-
-    for j in range(2):
-        recvbuf[j] = camps[clamp(ids_smem[0, 0, j], blocks)]
-
     send_weights(0)
     load_users.wait()
     swap_users.wait()
@@ -304,7 +303,7 @@
     first_at = [columns.index(e) * clusters for e in range(fan)]
     second_at = [(columns.index(e, fan)) * clusters for e in range(fan)]
 
-    @pl.loop(0, clusters, unroll=4)
+    @pl.loop(0, clusters, unroll=8)
     def _(k):
         emb = jnp.concatenate(
             [recvbuf[clamp(
@@ -327,9 +326,8 @@
             kmat[k, at, :] = jnp.exp2(raw * wide_scale * camp_scale).astype(jnp.bfloat16)
 
     def split(x):
-        upper = x.astype(jnp.bfloat16)
-        lower = (x - upper.astype(jnp.float32)).astype(jnp.bfloat16)
-        return jnp.concatenate([upper, lower], axis=0)
+        upper = x.astype(bf16).astype(f32)
+        return jnp.concatenate([upper, x - upper], axis=0).astype(bf16)
 
     part = fan * clusters // 2
     group = clusters // 2
@@ -344,17 +342,17 @@
         picked = pick(to_items[...], rows)
         a, b, c, d = [picked[p * part:(p + 1) * part] for p in range(4)]
         table = jnp.where(left, a + pltpu.roll(d, half, 1), c + pltpu.roll(b, half, 1))
-        return split(jnp.concatenate(
-            [table[p * clusters:(p + 1) * clusters] for p in range(fan // 2)], axis=1))
+        return jnp.concatenate(
+            [table[p * clusters:(p + 1) * clusters] for p in range(fan // 2)], axis=1)
 
     def partial_sums(v, h):
         at = h * group
+        lhs = split(v[at:at + group])
 
         def add(k, acc):
             out = lax.dot_general(
-                v, kmat[k], (((1,), (1,)), ((), ())), preferred_element_type=f32)
-            both = out[at:at + group] + out[clusters + at:clusters + at + group]
-            return acc + jnp.where(row_id == k - at, both, 0.0)
+                lhs, kmat[k], (((1,), (1,)), ((), ())), preferred_element_type=f32)
+            return acc + jnp.where(row_id == k - at, out[:group] + out[group:], 0.0)
 
         zero = jnp.zeros((group, all_users), f32)
         return lax.fori_loop(at, at + group, add, zero, unroll=8)
@@ -374,9 +372,7 @@
             at = h * group
             swaps[h].wait()
             den = 1.0 + (own[h] + den_recv[step, at:at + group])
-            q = jnp.where(live_users[at:at + group], 1.0 / den, 0.0)
-            upper = q.astype(bf16).astype(f32)
-            q = jnp.concatenate([upper, q - upper], axis=0).astype(bf16)
+            q = split(jnp.where(live_users[at:at + group], 1.0 / den, 0.0))
 
             def add(k, acc, q=q, at=at):
                 out = jnp.dot(q, kmat[k], preferred_element_type=f32)

time: 111 us -> 110 us (level)
  no operation moved by 1% of the time
where the time goes in v5:
time: 110 us
  Pallas kernels  106 us (96%)
  local copies, waits for them, and re-layouts  2.85 us (3%)
    pallas_call x1, Pallas kernels, body(): pl.pallas_call(functools.partial(kernel, radix), out_shape=(jax.ShapeDtyp...  106 us
    unnamed x2, local copies, waits for them, and re-layouts  2.85 us

profile of v5, /device:TPU:1, one launch (start us, length us, event | category | flops | bytes accessed | tf_op | source)
XLA Modules:
  0.0 109.6 jit_solution(8109863565305494349)
XLA Ops:
  0.6 106.1 %allocate.1 = (f32[16,512]{1,0:T(8,128)}, f32[128,128]{1,0:T(8,128)}) custom-call(s32[4,16]{1,0:T(4,128)} %bitcast.4, s32[4,16]{1,0:T(4,128)} %bitcast.5, s32[1,16]{1,0:T(1,128)} %bitcast.6, s32[1,128]{1,0:T(1,128)} %bitcast.7, f32[128,128]{1,0:T(8,128)} %init_hbm.1, f32[128,128]{1,0:T(8,128)} %limit_hbm.1, bf16[128,128,256]{2,1,0:T(8,128)(2,1)} %camp_hbm.1, ...), custom_call_target="tpu_custom_call" | custom-call | tf_op jit(solution)/shard_map/allocate/pallas_call | solution.py:454
  106.8 1.4 %copy.12 = f32[16,512]{1,0:T(8,128)} copy(f32[16,512]{1,0:T(8,128)} %get-tuple-element.4) | data formatting | bytes 65536
  108.1 1.5 %copy.13 = f32[128,128]{1,0:T(8,128)} copy(f32[128,128]{1,0:T(8,128)} %get-tuple-element.5) | data formatting | bytes 131072

commit v6 on v5

--- a/solution.py
+++ b/solution.py
@@ -263,10 +263,10 @@
     for d in bulk_order:
         for j in range(2):
             sendbuf[2 * d + j] = camps[clamp(ids_smem[d, 0, j], blocks)]
-        pair = pl.ds(2 * d, 2)
-        remote(
-            sendbuf.at[pair], recvbuf.at[pair], bulk_ssem, bulk_rsem, (partner(d, 1), rep)
-        ).start()
+            remote(
+                sendbuf.at[2 * d + j], recvbuf.at[2 * d + j], bulk_ssem, bulk_rsem,
+                (partner(d, 1), rep),
+            ).start()
 
     for j in range(2):
         recvbuf[j] = camps[clamp(ids_smem[0, 0, j], blocks)]

time: 110 us -> 110 us (level)
  no operation moved by 1% of the time
where the time goes in v6:
time: 110 us
  Pallas kernels  106 us (96%)
  local copies, waits for them, and re-layouts  2.85 us (3%)
    pallas_call x1, Pallas kernels, body(): pl.pallas_call(functools.partial(kernel, radix), out_shape=(jax.ShapeDtyp...  106 us
    unnamed x2, local copies, waits for them, and re-layouts  2.85 us

profile of v6, /device:TPU:1, one launch (start us, length us, event | category | flops | bytes accessed | tf_op | source)
XLA Modules:
  0.0 109.6 jit_solution(12829144328218600925)
XLA Ops:
  0.6 106.1 %allocate.1 = (f32[16,512]{1,0:T(8,128)}, f32[128,128]{1,0:T(8,128)}) custom-call(s32[4,16]{1,0:T(4,128)} %bitcast.4, s32[4,16]{1,0:T(4,128)} %bitcast.5, s32[1,16]{1,0:T(1,128)} %bitcast.6, s32[1,128]{1,0:T(1,128)} %bitcast.7, f32[128,128]{1,0:T(8,128)} %init_hbm.1, f32[128,128]{1,0:T(8,128)} %limit_hbm.1, bf16[128,128,256]{2,1,0:T(8,128)(2,1)} %camp_hbm.1, ...), custom_call_target="tpu_custom_call" | custom-call | tf_op jit(solution)/shard_map/allocate/pallas_call | solution.py:454
  106.8 1.4 %copy.12 = f32[16,512]{1,0:T(8,128)} copy(f32[16,512]{1,0:T(8,128)} %get-tuple-element.4) | data formatting | bytes 65536
  108.2 1.5 %copy.13 = f32[128,128]{1,0:T(8,128)} copy(f32[128,128]{1,0:T(8,128)} %get-tuple-element.5) | data formatting | bytes 131072
